TPU v7x, 128 devices: a whole 4x4x4 slice. The times are simulated.
128 devices in a mesh: dp: 8 (over z_lo, x), seq: 16 (over z_hi, y, core).
Axes of the slice: x: 4, y: 4, z: 4 (z_hi: 2, z_lo: 2; z = z_hi * 2 + z_lo), core: 2. Of those that a mesh axis runs over, the one named last changes fastest.
Arguments:
- series: bfloat16 [8, 8192, 128], P('dp', 'seq'), may hold values from -6 to 6
- cotangent: bfloat16 [8, 8192, 128], P('dp', 'seq'), may hold values from -6 to 6
- w_in: bfloat16 [128, 384], replicated, may hold values from -0.5 to 0.5
- w_out: bfloat16 [128, 128], replicated, may hold values from -0.5 to 0.5
- taps: float32 [3, 384], replicated, may hold values from -3 to 3
- skip_one: float32 [128], replicated, may hold values from 0.5 to 1.5
- skip_two: float32 [128], replicated, may hold values from 0.5 to 1.5
- filter_one: float32 [8, 8192], P(None, 'seq'), may hold values from -0.0625 to 0.0625
- filter_two: float32 [8, 8192], P(None, 'seq'), may hold values from -0.0625 to 0.0625
Outputs:
- output: bfloat16 [8, 8192, 128], P('dp', 'seq')
- d_series: bfloat16 [8, 8192, 128], P('dp', 'seq')
- grad_w_in: float32 [128, 384], replicated
- grad_w_out: float32 [128, 128], replicated
- grad_taps: float32 [3, 384], replicated
- grad_skip_one: float32 [128], replicated
- grad_skip_two: float32 [128], replicated
- grad_filter_one: float32 [8, 8192], P(None, 'seq')
- grad_filter_two: float32 [8, 8192], P(None, 'seq')
All inputs are finite; a program needn't handle non-finite values.
Results may differ from a plain program's by a relative error of at most 0.015.
Values may be sent and summed in bfloat16 or wider, within the bound.
A program may use at most 128 MiB of HBM per device.

v0:
```python
import math
import numpy as np
import jax
import jax.numpy as jnp
from jax import lax
from jax.sharding import PartitionSpec as P

HIGHEST = lax.Precision.HIGHEST
LANES = 128


def dft_tables(length):
    size = 2 * length
    rows = size // LANES
    half = length // LANES
    k1 = np.arange(rows)
    f1 = np.exp(-2j * np.pi * (np.outer(k1, np.arange(half)) % rows) / rows)
    turn = np.exp(-2j * np.pi * np.outer(k1, np.arange(LANES)) / size)
    f2 = np.exp(-2j * np.pi * (np.outer(np.arange(LANES), np.arange(LANES)) % LANES) / LANES)
    fwd1 = np.concatenate([f1.real, f1.imag], axis=0)
    fwd2 = np.block([[f2.real, f2.imag], [-f2.imag, f2.real]])
    inv2 = np.block([[f2.real, -f2.imag], [f2.imag, f2.real]])
    inv1 = np.concatenate([f1.real.T, f1.imag.T], axis=1) / size
    as32 = lambda a: jnp.asarray(np.asarray(a, np.float32))
    return {
        "rows": rows,
        "fwd1": as32(fwd1),
        "fwd2": as32(fwd2),
        "inv1": as32(inv1),
        "inv2": as32(inv2),
        "turn_r": as32(turn.real)[:, None, :],
        "turn_i": as32(turn.imag)[:, None, :],
    }


def spectrum(x, tab):
    rows = tab["rows"]
    a = jnp.einsum("kn,ncm->kcm", tab["fwd1"], x, precision=HIGHEST)
    ar, ai = (a[:rows], a[rows:])
    tr, ti = (tab["turn_r"], tab["turn_i"])
    cat = jnp.concatenate([ar * tr - ai * ti, ar * ti + ai * tr], axis=-1)
    return jnp.einsum("kcm,mj->kcj", cat, tab["fwd2"], precision=HIGHEST)


def signal(s, tab):
    b = jnp.einsum("kcj,jm->kcm", s, tab["inv2"], precision=HIGHEST)
    br, bi = (b[..., :LANES], b[..., LANES:])
    tr, ti = (tab["turn_r"], tab["turn_i"])
    stacked = jnp.concatenate([br * tr + bi * ti, bi * tr - br * ti], axis=0)
    return jnp.einsum("nk,kcm->ncm", tab["inv1"], stacked, precision=HIGHEST)


def cmul(a, b, conj=False):
    ar, ai = (a[..., :LANES], a[..., LANES:])
    br, bi = (b[..., :LANES], b[..., LANES:])
    if conj:
        bi = -bi
    return jnp.concatenate([ar * br - ai * bi, ar * bi + ai * br], axis=-1)


def fold(x):
    c, length = x.shape
    return jnp.swapaxes(x.reshape(c, length // LANES, LANES), 0, 1)


def unfold(x):
    half, c, lanes = x.shape
    return jnp.swapaxes(x, 0, 1).reshape(c, half * lanes)


def shards(series, cotangent, w_in, w_out, taps, skip_one, skip_two, filter_one, filter_two):
    _, block, width = series.shape
    seq_n = lax.axis_size("seq")
    dp_n = lax.axis_size("dp")
    length = block * seq_n
    half = length // LANES
    me = lax.axis_index("seq")
    per = width // seq_n
    filters = filter_one.shape[0]
    group_width = width // filters
    per_group = group_width // per
    group = me // per_group
    grad_scale = 1.0 / math.sqrt(dp_n * series.shape[0] * length)
    tab = dft_tables(length)
    rows_sent = jnp.repeat(
        jnp.swapaxes(jnp.stack([filter_one, filter_two]), 0, 1), per_group, axis=0
    )
    rows_got = lax.all_to_all(rows_sent, "seq", 0, 0, tiled=True)
    h_rows = jnp.swapaxes(rows_got, 0, 1).reshape(2, length)
    taps_sel = lax.dynamic_index_in_dim(
        taps.reshape(3, 3, seq_n, per), me, axis=2, keepdims=False
    ).reshape(3, 3 * per)
    skip1 = lax.dynamic_index_in_dim(skip_one.reshape(seq_n, per), me, axis=0, keepdims=False)
    skip2 = lax.dynamic_index_in_dim(skip_two.reshape(seq_n, per), me, axis=0, keepdims=False)
    skip1 = skip1[None, :, None]
    skip2 = skip2[None, :, None]
    proj_blk = jnp.einsum("td,dc->ct", series[0], w_in, preferred_element_type=jnp.float32)
    proj_blk = lax.all_to_all(proj_blk.reshape(3, seq_n, per, block), "seq", 1, 1, tiled=True)
    proj = jnp.swapaxes(proj_blk, 1, 2).reshape(3 * per, length)
    prev1 = jnp.pad(proj, ((0, 0), (1, 0)))[:, :length]
    prev2 = jnp.pad(proj, ((0, 0), (2, 0)))[:, :length]
    conv = taps_sel[0][:, None] * proj + taps_sel[1][:, None] * prev1 + taps_sel[2][:, None] * prev2
    conv_f = fold(conv)
    value = conv_f[:, :per]
    gate_one = conv_f[:, per : 2 * per]
    gate_two = conv_f[:, 2 * per :]
    h_spec = spectrum(fold(h_rows), tab)
    h_one = h_spec[:, 0:1]
    h_two = h_spec[:, 1:2]
    v_spec = spectrum(value, tab)
    y_one = signal(cmul(v_spec, h_one), tab) + skip1 * value
    gated_mid = gate_one * y_one
    m_spec = spectrum(gated_mid, tab)
    y_two = signal(cmul(m_spec, h_two), tab) + skip2 * gated_mid
    product = (gate_two * y_two).astype(jnp.bfloat16)
    dprod_blk = jnp.einsum("td,cd->ct", cotangent[0], w_out, preferred_element_type=jnp.float32)
    dprod_blk = lax.all_to_all(dprod_blk.reshape(seq_n, per, block), "seq", 0, 0, tiled=True)
    d_product = jnp.swapaxes(dprod_blk.reshape(seq_n, per, block // LANES, LANES), 1, 2).reshape(
        half, per, LANES
    )
    grad_two = d_product * gate_two
    d_gate_two = d_product * y_two
    g2_spec = spectrum(grad_two, tab)
    d_mid = signal(cmul(g2_spec, h_two, conj=True), tab) + skip2 * grad_two
    grad_one = d_mid * gate_one
    d_gate_one = d_mid * y_one
    g1_spec = spectrum(grad_one, tab)
    d_value = signal(cmul(g1_spec, h_one, conj=True), tab) + skip1 * grad_one
    corr = jnp.concatenate(
        [
            jnp.sum(cmul(g1_spec, v_spec, conj=True), axis=1, keepdims=True),
            jnp.sum(cmul(g2_spec, m_spec, conj=True), axis=1, keepdims=True),
        ],
        axis=1,
    )
    filt_grad = unfold(signal(corr, tab))
    d_conv = unfold(jnp.concatenate([d_value, d_gate_one, d_gate_two], axis=1))
    next1 = jnp.pad(d_conv, ((0, 0), (0, 1)))[:, 1:]
    next2 = jnp.pad(d_conv, ((0, 0), (0, 2)))[:, 2:]
    d_proj = (
        taps_sel[0][:, None] * d_conv + taps_sel[1][:, None] * next1 + taps_sel[2][:, None] * next2
    ).astype(jnp.bfloat16)
    local_taps = jnp.stack(
        [
            jnp.sum(d_conv * proj, axis=1),
            jnp.sum(d_conv * prev1, axis=1),
            jnp.sum(d_conv * prev2, axis=1),
        ]
    )
    local_skip1 = jnp.sum(grad_one * value, axis=(0, 2))
    local_skip2 = jnp.sum(grad_two * gated_mid, axis=(0, 2))
    prod_blocks = product.reshape(seq_n, half // seq_n, per, LANES)
    prod_blocks = lax.all_to_all(prod_blocks, "seq", 0, 0, tiled=True)
    output = jnp.einsum(
        "jnim,jid->nmd",
        prod_blocks,
        w_out.reshape(seq_n, per, width),
        preferred_element_type=jnp.float32,
    ).astype(jnp.bfloat16)
    output = output.reshape(1, block, width)
    dp_blocks = d_proj.reshape(3, per, seq_n, block)
    dp_blocks = lax.all_to_all(dp_blocks, "seq", 2, 2, tiled=True)
    d_series = jnp.einsum(
        "pijt,dpji->td",
        dp_blocks,
        w_in.reshape(width, 3, seq_n, per),
        preferred_element_type=jnp.float32,
    ).astype(jnp.bfloat16)
    d_series = d_series.reshape(1, block, width)
    fg_blocks = lax.all_to_all(filt_grad.reshape(2, seq_n, block), "seq", 1, 1, tiled=True)
    fg_blocks = jnp.sum(fg_blocks.reshape(2, filters, per_group, block), axis=2)
    prod_rows = jnp.transpose(prod_blocks, (1, 3, 0, 2)).reshape(block, width)
    dp_rows = jnp.transpose(dp_blocks, (3, 0, 2, 1)).reshape(block, 3 * width)
    local_w_in = jnp.einsum("td,tc->dc", series[0], dp_rows, preferred_element_type=jnp.float32)
    local_w_out = jnp.einsum(
        "tc,td->cd", prod_rows, cotangent[0], preferred_element_type=jnp.float32
    )
    small = jnp.concatenate(
        [
            local_taps.reshape(3, 3, 1, per),
            jnp.stack([local_skip1, local_skip2, jnp.zeros_like(local_skip1)]).reshape(
                3, 1, 1, per
            ),
        ],
        axis=1,
    )
    small_full = jnp.zeros((3, 4, seq_n, per), jnp.float32)
    small_full = lax.dynamic_update_slice(small_full, small, (0, 0, me, 0))
    grad_w_in, grad_w_out, small_full = lax.psum(
        (local_w_in, local_w_out, small_full), ("dp", "seq")
    )
    fg_blocks = lax.psum(fg_blocks, "dp")
    small_full = small_full.reshape(3, 4, width)
    grad_taps = small_full[:, :3].reshape(3, 3 * width)
    grad_skip_one = small_full[0, 3]
    grad_skip_two = small_full[1, 3]
    return (
        output,
        d_series,
        grad_scale * grad_w_in,
        grad_scale * grad_w_out,
        grad_scale * grad_taps,
        grad_scale * grad_skip_one,
        grad_scale * grad_skip_two,
        grad_scale * fg_blocks[0],
        grad_scale * fg_blocks[1],
    )


def solution(mesh):
    in_specs = (
        P("dp", "seq", None),
        P("dp", "seq", None),
        P(),
        P(),
        P(),
        P(),
        P(),
        P(None, "seq"),
        P(None, "seq"),
    )
    out_specs = (
        P("dp", "seq", None),
        P("dp", "seq", None),
        P(),
        P(),
        P(),
        P(),
        P(),
        P(None, "seq"),
        P(None, "seq"),
    )
    return jax.shard_map(shards, mesh=mesh, in_specs=in_specs, out_specs=out_specs, check_vma=False)
```

profile of v0, /device:TPU:1, one launch (start us, length us, event | category | flops | bytes accessed | tf_op | source)
XLA Modules:
  0.0 364.3 jit_solution(12172871343249868817)
XLA Ops:
  8.6 9.4 %all-to-all-start.1 = ((f32[16,2,512]{2,1,0:T(2,128)}), f32[16,2,512]{2,1,0:T(2,128)S(1)}, u32[]{:S(2)}, u32[]{:S(2)}) async-start(f32[16,2,512]{2,1,0:T(2,128)} %bitcast.12), calls=%async_computation.1 | async-start | bytes 131072 | tf_op jit(solution)/shard_map/all_to_all | solution.py:88
  20.6 1.2 fusion.68
  22.7 2.7 all-to-all-done.1
  25.4 4.6 %all-to-all-start.3 = ((f32[16,8,512]{2,1,0:T(8,128)}), f32[16,8,512]{2,1,0:T(8,128)S(1)}, u32[]{:S(2)}, u32[]{:S(2)}) async-start(f32[16,8,512]{2,1,0:T(8,128)} %fusion.70), calls=%async_computation.3 | async-start | bytes 524288 | tf_op jit(solution)/shard_map/all_to_all | solution.py:117
  31.8 6.9 %all-to-all-done.3 = f32[16,8,512]{2,1,0:T(8,128)S(1)} async-done(((f32[16,8,512]{2,1,0:T(8,128)}), f32[16,8,512]{2,1,0:T(8,128)S(1)}, u32[]{:S(2)}, u32[]{:S(2)}) %all-to-all-start.3) | async-done | bytes 262176 | tf_op jit(solution)/shard_map/all_to_all | solution.py:117
  38.7 4.2 %all-to-all-start = ((f32[3,16,8,512]{3,2,0,1:T(8,128)}), f32[3,16,8,512]{3,2,0,1:T(8,128)S(1)}, u32[]{:S(2)}, u32[]{:S(2)}) async-start(f32[3,16,8,512]{3,2,0,1:T(8,128)} %fusion.68), calls=%async_computation | async-start | bytes 1572864 | tf_op jit(solution)/shard_map/all_to_all | solution.py:98
  43.6 13.9 %all-to-all-done = f32[3,16,8,512]{3,2,0,1:T(8,128)S(1)} async-done(((f32[3,16,8,512]{3,2,0,1:T(8,128)}), f32[3,16,8,512]{3,2,0,1:T(8,128)S(1)}, u32[]{:S(2)}, u32[]{:S(2)}) %all-to-all-start) | async-done | bytes 786464 | tf_op jit(solution)/shard_map/all_to_all | solution.py:98
  59.1 1.0 fusion.64
  60.2 1.0 fusion.102
  61.3 1.9 fusion.25
  64.1 1.1 fusion.29
  66.1 1.1 convolution_add_fusion.1
  67.3 1.0 fusion.101
  68.5 1.9 fusion.3
  70.4 2.0 fusion.36
  72.9 1.1 fusion.7
  74.0 1.1 fusion.40
  75.4 1.1 convolution_add_fusion.3
  76.5 1.0 fusion.100
  77.7 1.9 fusion.14
  79.8 1.1 fusion.18
  81.1 1.1 convolution_add_fusion
  82.2 1.2 multiply_reduce_fusion.3
  86.7 4.0 %all-to-all-start.5 = ((f32[2,16,512]{2,0,1:T(2,128)}), f32[2,16,512]{2,0,1:T(2,128)S(1)}, u32[]{:S(2)}, u32[]{:S(2)}) async-start(f32[2,16,512]{2,0,1:T(2,128)} %copy.198), calls=%async_computation.5 | async-start | bytes 131072 | tf_op jit(solution)/shard_map/all_to_all | solution.py:170
  91.5 67.0 %psum.30 = f32[3,4,128]{2,1,0:T(4,128)S(1)} all-reduce(f32[3,4,128]{2,1,0:T(4,128)S(1)} %reshape.136), channel_id=1, replica_groups=mesh['dp'=8,'seq'=16] {'dp','seq'}, use_global_device_ids=true, to_apply=%region_7.8 | all-reduce | flops 1536 | bytes 12288 | tf_op jit(solution)/shard_map/psum | solution.py:189
  160.2 1.0 copy.188
  161.9 4.3 %all-to-all-start.2 = ((bf16[16,4,8,128]{3,2,1,0:T(8,128)(2,1)}), bf16[16,4,8,128]{3,2,1,0:T(8,128)(2,1)S(1)}, u32[]{:S(2)}, u32[]{:S(2)}) async-start(bf16[16,4,8,128]{3,2,1,0:T(8,128)(2,1)} %copy.177), calls=%async_computation.2 | async-start | bytes 262144 | tf_op jit(solution)/shard_map/all_to_all | solution.py:153
  166.3 25.2 %psum.31 = f32[2,8,512]{2,0,1:T(2,128)S(1)} all-reduce(f32[2,8,512]{2,0,1:T(2,128)S(1)} %bitcast_reduce_fusion), channel_id=1, replica_groups=mesh['dp'=8,'seq'=16] {'dp'}, use_global_device_ids=true, to_apply=%region_11.12 | all-reduce | flops 8192 | bytes 65536 | tf_op jit(solution)/shard_map/psum | solution.py:192
  192.7 14.6 %all-to-all-start.4 = ((bf16[3,8,16,512]{3,1,0,2:T(8,128)(2,1)}), bf16[3,8,16,512]{3,1,0,2:T(8,128)(2,1)S(1)}, u32[]{:S(2)}, u32[]{:S(2)}) async-start(bf16[3,8,16,512]{3,1,0,2:T(8,128)(2,1)} %copy.188), calls=%async_computation.4 | async-start | bytes 786432 | tf_op jit(solution)/shard_map/all_to_all | solution.py:162
  209.0 8.0 %all-to-all-done.4 = bf16[3,8,16,512]{3,1,0,2:T(8,128)(2,1)S(1)} async-done(((bf16[3,8,16,512]{3,1,0,2:T(8,128)(2,1)}), bf16[3,8,16,512]{3,1,0,2:T(8,128)(2,1)S(1)}, u32[]{:S(2)}, u32[]{:S(2)}) %all-to-all-start.4) | async-done | bytes 393248 | tf_op jit(solution)/shard_map/all_to_all | solution.py:162
  218.1 1.0 fusion.2
  219.0 136.0 %all-reduce.7.cloned.1.call-done = (f32[128,384]{0,1:T(8,128)}, f32[128,128]{1,0:T(8,128)}) async-done(((f32[128,384]{0,1:T(8,128)}, f32[128,128]{1,0:T(8,128)}), (f32[128,384]{0,1:T(8,128)}, f32[128,128]{1,0:T(8,128)})) %all-reduce.7.cloned.1.call-update) | async-done | bytes 262160 | tf_op jit(solution)/shard_map/psum | solution.py:189
  (105 shorter events, 25.0 us)
Async XLA Ops:
  7.2 13.4 %copy-start = (bf16[1,512,128]{2,1,0:T(8,128)(2,1)S(1)}, bf16[1,512,128]{2,1,0:T(8,128)(2,1)}, u32[]{:S(2)}) copy-start(bf16[1,512,128]{2,1,0:T(8,128)(2,1)} %param.15) | copy-start | bytes 393220
  8.6 10.5 %copy-start.8 = (bf16[128,384]{1,0:T(8,128)(2,1)S(1)}, bf16[128,384]{1,0:T(8,128)(2,1)}, u32[]{:S(2)}) copy-start(bf16[128,384]{1,0:T(8,128)(2,1)} %param.17) | copy-start | bytes 294916
  8.6 16.8 %all-to-all-start.1 = ((f32[16,2,512]{2,1,0:T(2,128)}), f32[16,2,512]{2,1,0:T(2,128)S(1)}, u32[]{:S(2)}, u32[]{:S(2)}) async-start(f32[16,2,512]{2,1,0:T(2,128)} %bitcast.12), calls=%async_computation.1 | async-start | bytes 131072 | tf_op jit(solution)/shard_map/all_to_all | solution.py:88
  18.1 0.7 copy-start.11
  19.2 0.7 copy-start.12
  19.8 0.7 copy-start.13
  20.6 1.2 copy-start.7
  20.6 1.2 copy-start.10
  25.4 13.3 %all-to-all-start.3 = ((f32[16,8,512]{2,1,0:T(8,128)}), f32[16,8,512]{2,1,0:T(8,128)S(1)}, u32[]{:S(2)}, u32[]{:S(2)}) async-start(f32[16,8,512]{2,1,0:T(8,128)} %fusion.70), calls=%async_computation.3 | async-start | bytes 524288 | tf_op jit(solution)/shard_map/all_to_all | solution.py:117
  30.0 0.8 copy-start.6
  30.8 0.8 copy-start.3
  30.8 0.9 copy-start.4
  31.7 11.1 %copy-start.2 = (f32[256,256,1]{1,0,2:T(8,128)S(1)}, f32[256,256,1]{1,0,2:T(8,128)}, u32[]{:S(2)}) copy-start(f32[256,256,1]{1,0,2:T(8,128)} %constant.59) | copy-start | bytes 786436
  38.7 18.8 %all-to-all-start = ((f32[3,16,8,512]{3,2,0,1:T(8,128)}), f32[3,16,8,512]{3,2,0,1:T(8,128)S(1)}, u32[]{:S(2)}, u32[]{:S(2)}) async-start(f32[3,16,8,512]{3,2,0,1:T(8,128)} %fusion.68), calls=%async_computation | async-start | bytes 1572864 | tf_op jit(solution)/shard_map/all_to_all | solution.py:98
  63.2 1.0 copy-start.1
  65.3 0.8 copy-start.5
  86.7 75.3 %all-to-all-start.5 = ((f32[2,16,512]{2,0,1:T(2,128)}), f32[2,16,512]{2,0,1:T(2,128)S(1)}, u32[]{:S(2)}, u32[]{:S(2)}) async-start(f32[2,16,512]{2,0,1:T(2,128)} %copy.198), calls=%async_computation.5 | async-start | bytes 131072 | tf_op jit(solution)/shard_map/all_to_all | solution.py:170
  161.9 30.8 %all-to-all-start.2 = ((bf16[16,4,8,128]{3,2,1,0:T(8,128)(2,1)}), bf16[16,4,8,128]{3,2,1,0:T(8,128)(2,1)S(1)}, u32[]{:S(2)}, u32[]{:S(2)}) async-start(bf16[16,4,8,128]{3,2,1,0:T(8,128)(2,1)} %copy.177), calls=%async_computation.2 | async-start | bytes 262144 | tf_op jit(solution)/shard_map/all_to_all | solution.py:153
  192.7 24.4 %all-to-all-start.4 = ((bf16[3,8,16,512]{3,1,0,2:T(8,128)(2,1)}), bf16[3,8,16,512]{3,1,0,2:T(8,128)(2,1)S(1)}, u32[]{:S(2)}, u32[]{:S(2)}) async-start(bf16[3,8,16,512]{3,1,0,2:T(8,128)(2,1)} %copy.188), calls=%async_computation.4 | async-start | bytes 786432 | tf_op jit(solution)/shard_map/all_to_all | solution.py:162
  207.3 147.7 %all-reduce.7.cloned.1.call-start = ((), (), s32[]{:S(2)}) async-start(), calls=%async_computation.6 | async-start | bytes 524288 | tf_op jit(solution)/shard_map/psum | solution.py:189
  356.0 0.8 copy-start.9
Sparse Core Ops, SparseCore 0:
  218.2 136.7 all-reduce.6
where the time goes:
time: 365 us; the launch traced here: 364 us
  waiting for transfers between devices  168 us (46%)
  blocking collectives  92.2 us (25%)
  starting transfers between devices  41.2 us (11%)
  matrix products  28.5 us (8%)
  between operations  14.5 us (4%)
  local copies, waits for them, and re-layouts  13.5 us (4%)
  other arithmetic  6.89 us (2%)
    psum x1, waiting for transfers between devices, shards(): lax.psum((local_w_in, local_w_out, small_full), ('dp', 'seq'))  136 us
    psum x1, blocking collectives, shards(): lax.psum((local_w_in, local_w_out, small_full), ('dp', 'seq'))  67 us
    psum x1, blocking collectives, shards(): fg_blocks = lax.psum(fg_blocks, 'dp')  25.2 us
    all_to_all x1, starting transfers between devices, shards(): dp_blocks = lax.all_to_all(dp_blocks, 'seq', 2, 2, tiled=True)  14.6 us
    all_to_all x1, waiting for transfers between devices, shards(): lax.all_to_all(proj_blk.reshape(3, seq_n, per, block), 'seq', 1, 1, tiled...  13.9 us
    all_to_all x1, starting transfers between devices, shards(): rows_got = lax.all_to_all(rows_sent, 'seq', 0, 0, tiled=True)  9.43 us
    unnamed x37, local copies, waits for them, and re-layouts  8.79 us
    dot_general x5, matrix products, spectrum(): return jnp.einsum('kcm,mj->kcj', cat, tab['fwd2'], precision=HIGHEST)  8.23 us
  transfers between devices with their start and end apart: 7, of which 5 were waited for; matrix products, arithmetic and copies ran while one was open for 3% of the time, Pallas kernels for 0%

commit v1 on v0

--- a/solution.py
+++ b/solution.py
@@ -187,7 +187,7 @@
     small_full = jnp.zeros((3, 4, seq_n, per), jnp.float32)
     small_full = lax.dynamic_update_slice(small_full, small, (0, 0, me, 0))
     grad_w_in, grad_w_out, small_full = lax.psum(
-        (local_w_in, local_w_out, small_full), ("dp", "seq")
+        lax.psum((local_w_in, local_w_out, small_full), "seq"), "dp"
     )
     fg_blocks = lax.psum(fg_blocks, "dp")
     small_full = small_full.reshape(3, 4, width)

time: 365 us -> 441 us (1.21)
  waiting for transfers between devices: 168 us -> 234 us
  starting transfers between devices: 41.2 us -> 46.4 us
    psum x1 -> x2, waiting for transfers between devices: 136 us -> 201 us  [the longest x1 129 us: shards(): lax.psum((local_w_in, local_w_out, small_full), 'seq')]
    all_to_all x1, starting transfers between devices: 4.33 us -> 9.25 us  [shards(): prod_blocks = lax.all_to_all(prod_blocks, 'seq', 0, 0, tiled=True)]
  transfers between devices with their start and end apart: 7 -> 8, of which waited for: 5 -> 6; matrix products, arithmetic and copies ran while one was open for 3% -> 3% of each run, Pallas kernels for 0% -> 0%
where the time goes in v1:
time: 441 us; the launch traced here: 436 us
  waiting for transfers between devices  234 us (53%)
  blocking collectives  92.4 us (21%)
  starting transfers between devices  46.4 us (11%)
  matrix products  28.5 us (6%)
  between operations  14.6 us (3%)
  local copies, waits for them, and re-layouts  13.5 us (3%)
  other arithmetic  6.89 us (2%)
    psum x1, waiting for transfers between devices, shards(): lax.psum((local_w_in, local_w_out, small_full), 'seq')  129 us
    psum x1, waiting for transfers between devices, shards(): lax.psum(lax.psum((local_w_in, local_w_out, small_full), 'seq'), 'dp')  71.8 us
    psum x1, blocking collectives, shards(): lax.psum((local_w_in, local_w_out, small_full), 'seq')  65.2 us
    psum x1, blocking collectives, shards(): lax.psum(lax.psum((local_w_in, local_w_out, small_full), 'seq'), 'dp')  27.2 us
    all_to_all x1, starting transfers between devices, shards(): dp_blocks = lax.all_to_all(dp_blocks, 'seq', 2, 2, tiled=True)  14.9 us
    all_to_all x1, waiting for transfers between devices, shards(): lax.all_to_all(proj_blk.reshape(3, seq_n, per, block), 'seq', 1, 1, tiled...  13.9 us
    all_to_all x1, starting transfers between devices, shards(): rows_got = lax.all_to_all(rows_sent, 'seq', 0, 0, tiled=True)  9.43 us
    all_to_all x1, starting transfers between devices, shards(): prod_blocks = lax.all_to_all(prod_blocks, 'seq', 0, 0, tiled=True)  9.25 us
  transfers between devices with their start and end apart: 8, of which 6 were waited for; matrix products, arithmetic and copies ran while one was open for 3% of the time, Pallas kernels for 0%

profile of v1, /device:TPU:1, one launch (start us, length us, event | category | flops | bytes accessed | tf_op | source)
XLA Modules:
  0.0 436.0 jit_solution(1665334850825399937)
XLA Ops:
  8.6 9.4 %all-to-all-start.1 = ((f32[16,2,512]{2,1,0:T(2,128)}), f32[16,2,512]{2,1,0:T(2,128)S(1)}, u32[]{:S(2)}, u32[]{:S(2)}) async-start(f32[16,2,512]{2,1,0:T(2,128)} %bitcast.12), calls=%async_computation.1 | async-start | bytes 131072 | tf_op jit(solution)/shard_map/all_to_all | solution.py:88
  20.6 1.2 fusion.68
  22.7 2.7 all-to-all-done.1
  25.4 4.6 %all-to-all-start.3 = ((f32[16,8,512]{2,1,0:T(8,128)}), f32[16,8,512]{2,1,0:T(8,128)S(1)}, u32[]{:S(2)}, u32[]{:S(2)}) async-start(f32[16,8,512]{2,1,0:T(8,128)} %fusion.70), calls=%async_computation.3 | async-start | bytes 524288 | tf_op jit(solution)/shard_map/all_to_all | solution.py:117
  31.8 6.9 %all-to-all-done.3 = f32[16,8,512]{2,1,0:T(8,128)S(1)} async-done(((f32[16,8,512]{2,1,0:T(8,128)}), f32[16,8,512]{2,1,0:T(8,128)S(1)}, u32[]{:S(2)}, u32[]{:S(2)}) %all-to-all-start.3) | async-done | bytes 262176 | tf_op jit(solution)/shard_map/all_to_all | solution.py:117
  38.7 4.2 all-to-all-start
  43.6 13.9 %all-to-all-done = f32[3,16,8,512]{3,2,0,1:T(8,128)S(1)} async-done(((f32[3,16,8,512]{3,2,0,1:T(8,128)}), f32[3,16,8,512]{3,2,0,1:T(8,128)S(1)}, u32[]{:S(2)}, u32[]{:S(2)}) %all-to-all-start) | async-done | bytes 786464 | tf_op jit(solution)/shard_map/all_to_all | solution.py:98
  59.1 1.0 fusion.64
  60.2 1.0 fusion.102
  61.3 1.9 fusion.25
  64.1 1.1 fusion.29
  66.1 1.1 convolution_add_fusion.1
  67.3 1.0 fusion.101
  68.5 1.9 fusion.3
  70.4 2.0 fusion.36
  72.9 1.1 fusion.7
  74.0 1.1 fusion.40
  75.4 1.1 convolution_add_fusion.3
  76.5 1.0 fusion.100
  77.7 1.9 fusion.14
  79.8 1.1 fusion.18
  81.1 1.1 convolution_add_fusion
  82.2 1.2 multiply_reduce_fusion.3
  86.7 4.0 all-to-all-start.5
  91.9 65.2 %psum.53 = f32[3,4,16,8]{3,2,1,0:T(8,128)S(1)} all-reduce(f32[3,4,16,8]{3,2,1,0:T(8,128)S(1)} %dynamic_update_slice.3), channel_id=1, replica_groups=mesh['dp'=8,'seq'=16] {'seq'}, use_global_device_ids=true, to_apply=%region_9.10 | all-reduce | flops 1536 | bytes 12288 | tf_op jit(solution)/shard_map/psum | solution.py:190
  159.0 9.3 %all-to-all-start.2 = ((bf16[16,4,8,128]{3,2,1,0:T(8,128)(2,1)}), bf16[16,4,8,128]{3,2,1,0:T(8,128)(2,1)S(1)}, u32[]{:S(2)}, u32[]{:S(2)}) async-start(bf16[16,4,8,128]{3,2,1,0:T(8,128)(2,1)} %copy.177), calls=%async_computation.2 | async-start | bytes 262144 | tf_op jit(solution)/shard_map/all_to_all | solution.py:153
  168.3 27.2 %all-reduce.5 = (f32[3,4,128]{2,1,0:T(4,128)S(1)}, f32[2,8,512]{2,0,1:T(2,128)S(1)}) all-reduce(f32[3,4,128]{2,1,0:T(4,128)S(1)} %reshape.136, f32[2,8,512]{2,0,1:T(2,128)S(1)} %bitcast_reduce_fusion), channel_id=1, replica_groups=mesh['dp'=8,'seq'=16] {'dp'}, use_global_device_ids=true, to_apply=%region_10.11 | all-reduce | flops 9728 | bytes 77824 | tf_op jit(solution)/shard_map/psum | solution.py:189
  195.5 14.9 %all-to-all-start.4 = ((bf16[3,8,16,512]{3,1,0,2:T(8,128)(2,1)}), bf16[3,8,16,512]{3,1,0,2:T(8,128)(2,1)S(1)}, u32[]{:S(2)}, u32[]{:S(2)}) async-start(bf16[3,8,16,512]{3,1,0,2:T(8,128)(2,1)} %copy.188), calls=%async_computation.4 | async-start | bytes 786432 | tf_op jit(solution)/shard_map/all_to_all | solution.py:162
  211.2 8.9 %all-to-all-done.4 = bf16[3,8,16,512]{3,1,0,2:T(8,128)(2,1)S(1)} async-done(((bf16[3,8,16,512]{3,1,0,2:T(8,128)(2,1)}), bf16[3,8,16,512]{3,1,0,2:T(8,128)(2,1)S(1)}, u32[]{:S(2)}, u32[]{:S(2)}) %all-to-all-start.4) | async-done | bytes 393248 | tf_op jit(solution)/shard_map/all_to_all | solution.py:162
  224.4 129.5 %all-reduce.10.cloned.1.call-done = (f32[128,384]{0,1:T(8,128)}, f32[128,128]{1,0:T(8,128)}) async-done(((f32[128,384]{0,1:T(8,128)}, f32[128,128]{1,0:T(8,128)}), (f32[128,384]{0,1:T(8,128)}, f32[128,128]{1,0:T(8,128)})) %all-reduce.10.cloned.1.call-update) | async-done | bytes 262160 | tf_op jit(solution)/shard_map/psum | solution.py:190
  353.9 1.0 fusion.2
  354.9 71.8 %all-reduce.12.cloned.1.call-done = (f32[128,384]{0,1:T(8,128)}, f32[128,128]{1,0:T(8,128)}) async-done(((f32[128,384]{0,1:T(8,128)}, f32[128,128]{1,0:T(8,128)}), (f32[128,384]{0,1:T(8,128)}, f32[128,128]{1,0:T(8,128)})) %all-reduce.12.cloned.1.call-update) | async-done | bytes 262160 | tf_op jit(solution)/shard_map/psum | solution.py:189
  (108 shorter events, 26.0 us)
Async XLA Ops:
  7.2 13.4 %copy-start = (bf16[1,512,128]{2,1,0:T(8,128)(2,1)S(1)}, bf16[1,512,128]{2,1,0:T(8,128)(2,1)}, u32[]{:S(2)}) copy-start(bf16[1,512,128]{2,1,0:T(8,128)(2,1)} %param.15) | copy-start | bytes 393220
  8.6 10.5 %copy-start.8 = (bf16[128,384]{1,0:T(8,128)(2,1)S(1)}, bf16[128,384]{1,0:T(8,128)(2,1)}, u32[]{:S(2)}) copy-start(bf16[128,384]{1,0:T(8,128)(2,1)} %param.17) | copy-start | bytes 294916
  8.6 16.8 %all-to-all-start.1 = ((f32[16,2,512]{2,1,0:T(2,128)}), f32[16,2,512]{2,1,0:T(2,128)S(1)}, u32[]{:S(2)}, u32[]{:S(2)}) async-start(f32[16,2,512]{2,1,0:T(2,128)} %bitcast.12), calls=%async_computation.1 | async-start | bytes 131072 | tf_op jit(solution)/shard_map/all_to_all | solution.py:88
  18.1 0.7 copy-start.11
  19.2 0.7 copy-start.12
  19.8 0.7 copy-start.13
  20.6 1.2 copy-start.7
  20.6 1.2 copy-start.10
  25.4 13.3 %all-to-all-start.3 = ((f32[16,8,512]{2,1,0:T(8,128)}), f32[16,8,512]{2,1,0:T(8,128)S(1)}, u32[]{:S(2)}, u32[]{:S(2)}) async-start(f32[16,8,512]{2,1,0:T(8,128)} %fusion.70), calls=%async_computation.3 | async-start | bytes 524288 | tf_op jit(solution)/shard_map/all_to_all | solution.py:117
  30.0 0.8 copy-start.6
  30.8 0.8 copy-start.3
  30.8 0.9 copy-start.4
  31.8 11.1 %copy-start.2 = (f32[256,256,1]{1,0,2:T(8,128)S(1)}, f32[256,256,1]{1,0,2:T(8,128)}, u32[]{:S(2)}) copy-start(f32[256,256,1]{1,0,2:T(8,128)} %constant.59) | copy-start | bytes 786436
  38.7 18.8 %all-to-all-start = ((f32[3,16,8,512]{3,2,0,1:T(8,128)}), f32[3,16,8,512]{3,2,0,1:T(8,128)S(1)}, u32[]{:S(2)}, u32[]{:S(2)}) async-start(f32[3,16,8,512]{3,2,0,1:T(8,128)} %fusion.68), calls=%async_computation | async-start | bytes 1572864 | tf_op jit(solution)/shard_map/all_to_all | solution.py:98
  63.2 1.0 copy-start.1
  65.3 0.8 copy-start.5
  86.7 72.4 %all-to-all-start.5 = ((f32[2,16,512]{2,0,1:T(2,128)}), f32[2,16,512]{2,0,1:T(2,128)S(1)}, u32[]{:S(2)}, u32[]{:S(2)}) async-start(f32[2,16,512]{2,0,1:T(2,128)} %copy.198), calls=%async_computation.5 | async-start | bytes 131072 | tf_op jit(solution)/shard_map/all_to_all | solution.py:170
  159.0 36.5 %all-to-all-start.2 = ((bf16[16,4,8,128]{3,2,1,0:T(8,128)(2,1)}), bf16[16,4,8,128]{3,2,1,0:T(8,128)(2,1)S(1)}, u32[]{:S(2)}, u32[]{:S(2)}) async-start(bf16[16,4,8,128]{3,2,1,0:T(8,128)(2,1)} %copy.177), calls=%async_computation.2 | async-start | bytes 262144 | tf_op jit(solution)/shard_map/all_to_all | solution.py:153
  195.5 24.6 %all-to-all-start.4 = ((bf16[3,8,16,512]{3,1,0,2:T(8,128)(2,1)}), bf16[3,8,16,512]{3,1,0,2:T(8,128)(2,1)S(1)}, u32[]{:S(2)}, u32[]{:S(2)}) async-start(bf16[3,8,16,512]{3,1,0,2:T(8,128)(2,1)} %copy.188), calls=%async_computation.4 | async-start | bytes 786432 | tf_op jit(solution)/shard_map/all_to_all | solution.py:162
  210.4 143.5 %all-reduce.10.cloned.1.call-start = ((), (), s32[]{:S(2)}) async-start(), calls=%async_computation.6 | async-start | bytes 524288 | tf_op jit(solution)/shard_map/psum | solution.py:190
  221.2 205.6 %all-reduce.12.cloned.1.call-start = ((), (), s32[]{:S(2)}) async-start(), calls=%async_computation.7 | async-start | bytes 524288 | tf_op jit(solution)/shard_map/psum | solution.py:189
  427.7 0.8 copy-start.9
Sparse Core Ops, SparseCore 0:
  221.3 132.5 all-reduce.9
  356.6 70.0 all-reduce.11
